TPU v7x, 32 devices: a whole 2x2x4 slice. The times are simulated.
32 devices in a mesh: tok: 4 (over z), hid: 8 (over y, x, core).
Axes of the slice: x: 2, y: 2, z: 4, core: 2. Of those that a mesh axis runs over, the one named last changes fastest.
Arguments:
- tokens: bfloat16 [2048, 1024], P('tok', 'hid'), may hold values from -6 to 6
- cotangent: bfloat16 [2048, 1024], P('tok', 'hid'), may hold values from -6 to 6
- frozen_in: bfloat16 [1024, 16384], P('tok', 'hid'), may hold values from -0.1875 to 0.1875
- frozen_out: bfloat16 [16384, 1024], P('hid', 'tok'), may hold values from -0.046875 to 0.046875
- input_adapter_first: bfloat16 [1024, 128], P('hid'), may hold values from -0.1875 to 0.1875
- input_adapter_second: bfloat16 [128, 16384], P(None, 'hid'), may hold values from -0.5 to 0.5
- adapter_out_a: bfloat16 [16384, 128], P('hid'), may hold values from -0.046875 to 0.046875
- adapter_out_b: bfloat16 [128, 1024], replicated, may hold values from -0.5 to 0.5
Outputs:
- input_gradient: float32 [2048, 1024], P('tok', 'hid')
- grad_in_a: float32 [1024, 128], P('hid')
- grad_in_b: float32 [128, 16384], P(None, 'hid')
- grad_out_a: float32 [16384, 128], P('hid')
- grad_out_b: float32 [128, 1024], P(None, 'hid')
All inputs are finite; a program needn't handle non-finite values.
Results may differ from a plain program's by a relative error of at most 0.0029.
Values may be sent and summed in bfloat16 or wider, within the bound.
A program may use at most 64 MiB of HBM per device.

v0:
```python
import math
import jax
import jax.numpy as jnp
from jax import lax
from jax.sharding import PartitionSpec as P

ADAPTER_SCALE = 0.5
GELU_K = 0.7978845608
GELU_C = 0.044715


def gelu_pair(pre_activation):
    tangent = jnp.tanh(
        GELU_K * (pre_activation + GELU_C * pre_activation * pre_activation * pre_activation)
    )
    value_out = 0.5 * pre_activation * (1.0 + tangent)
    slopes = 0.5 * (1.0 + tangent) + 0.5 * pre_activation * (1.0 - tangent * tangent) * GELU_K * (
        1.0 + 3.0 * GELU_C * pre_activation * pre_activation
    )
    return (value_out, slopes)


def local(
    tokens,
    cotangent,
    frozen_in,
    frozen_out,
    input_adapter_first,
    input_adapter_second,
    adapter_out_a,
    adapter_out_b,
):
    highest_precision = lax.Precision.HIGHEST
    device_local_rows = tokens.shape[0]
    rank_width = input_adapter_second.shape[0]
    gradient_scale = ADAPTER_SCALE / math.sqrt(device_local_rows * lax.axis_size("tok"))
    full_tokens, full_cotan = (
        lax.all_gather(tokens, "hid", axis=1, tiled=True),
        lax.all_gather(cotangent, "hid", axis=1, tiled=True),
    )
    in_rows = lax.all_gather(frozen_in, "tok", axis=0, tiled=True)
    in_a_full = lax.all_gather(input_adapter_first, "hid", axis=0, tiled=True)
    lowrank_input = jnp.dot(full_tokens, in_a_full, preferred_element_type=jnp.float32)
    second_float = input_adapter_second.astype(jnp.float32)
    out_a_float = adapter_out_a.astype(jnp.float32)
    pre_activation = jnp.dot(
        full_tokens, in_rows, preferred_element_type=jnp.float32
    ) + ADAPTER_SCALE * jnp.dot(lowrank_input, second_float, precision=highest_precision)
    value_out, slopes = gelu_pair(pre_activation)
    hidden_act = value_out.astype(jnp.bfloat16)
    backward_lowrank = jnp.einsum(
        "td,rd->tr", full_cotan, adapter_out_b, preferred_element_type=jnp.float32
    )
    rank_out = jnp.dot(hidden_act, adapter_out_a, preferred_element_type=jnp.float32)
    dense_backward = jnp.einsum(
        "td,fd->tf",
        full_cotan,
        lax.all_gather(frozen_out, "tok", axis=1, tiled=True),
        preferred_element_type=jnp.float32,
    )
    dense_backward = dense_backward + ADAPTER_SCALE * jnp.dot(
        backward_lowrank, out_a_float.T, precision=highest_precision
    )
    grad_pre = (dense_backward * slopes).astype(jnp.bfloat16)
    rank_backward = jnp.einsum(
        "tf,rf->tr", grad_pre, input_adapter_second, preferred_element_type=jnp.float32
    )
    dense_in = jnp.einsum("tf,df->td", grad_pre, in_rows, preferred_element_type=jnp.float32)
    grad_out_a = gradient_scale * jnp.dot(
        hidden_act.astype(jnp.float32).T, backward_lowrank, precision=highest_precision
    )
    grad_in_b = gradient_scale * jnp.dot(
        lowrank_input.T, grad_pre.astype(jnp.float32), precision=highest_precision
    )
    in_a_float = in_a_full.astype(jnp.float32)
    dx_term = dense_in + ADAPTER_SCALE * jnp.dot(
        rank_backward, in_a_float.T, precision=highest_precision
    )
    out_term = jnp.dot(rank_out.T, full_cotan.astype(jnp.float32), precision=highest_precision)
    in_term = jnp.dot(rank_backward.T, full_tokens.astype(jnp.float32), precision=highest_precision)
    rank_terms = jnp.concatenate([out_term, in_term], axis=0)
    input_gradient, rank_local = (
        lax.psum_scatter(dx_term, "hid", scatter_dimension=1, tiled=True),
        lax.psum_scatter(rank_terms, "hid", scatter_dimension=1, tiled=True),
    )
    grad_out_a, grad_in_b, rank_total = lax.psum((grad_out_a, grad_in_b, rank_local), "tok")
    grad_out_b = gradient_scale * rank_total[:rank_width]
    grad_in_a = gradient_scale * rank_total[rank_width:].T
    return (input_gradient, grad_in_a, grad_in_b, grad_out_a, grad_out_b)


def solution(mesh):
    in_specs = (
        P("tok", "hid"),
        P("tok", "hid"),
        P("tok", "hid"),
        P("hid", "tok"),
        P("hid", None),
        P(None, "hid"),
        P("hid", None),
        P(),
    )
    out_specs = (P("tok", "hid"), P("hid", None), P(None, "hid"), P("hid", None), P(None, "hid"))
    return jax.shard_map(local, mesh=mesh, in_specs=in_specs, out_specs=out_specs, check_vma=False)
```

profile of v0, /device:TPU:0, one launch (start us, length us, event | category | flops | bytes accessed | tf_op | source)
XLA Modules:
  0.0 421.3 jit_solution(1950593718763780741)
XLA Ops:
  10.0 11.0 %all_gather.19 = bf16[1024,128]{1,0:T(8,128)(2,1)S(1)} all-gather(bf16[128,128]{1,0:T(8,128)(2,1)} %param.12), channel_id=1, replica_groups=mesh['tok'=4,'hid'=8] {'hid'}, dimensions={0}, use_global_device_ids=true | all-gather | bytes 294912 | tf_op jit(solution)/shard_map/all_gather | solution.py:42
  21.0 15.1 %all-gather.5.cloned.1.call-done = bf16[512,1024]{1,0:T(8,128)(2,1)} async-done(((bf16[512,128]{1,0:T(8,128)(2,1)}), bf16[512,1024]{1,0:T(8,128)(2,1)}) %all-gather.5.cloned.1.call-update) | async-done | bytes 1048592 | tf_op jit(solution)/shard_map/all_gather | solution.py:39
  36.1 1.7 fusion.9
  37.8 23.7 %all-gather.9.cloned.1.call-done = bf16[512,1024]{1,0:T(8,128)(2,1)} async-done(((bf16[512,128]{1,0:T(8,128)(2,1)}), bf16[512,1024]{1,0:T(8,128)(2,1)}) %all-gather.9.cloned.1.call-update) | async-done | bytes 1048592 | tf_op jit(solution)/shard_map/all_gather | solution.py:38
  61.5 1.7 fusion.11
  63.2 80.7 %all-gather.11.cloned.1.call-done = bf16[1024,2048]{1,0:T(8,128)(2,1)} async-done(((bf16[256,2048]{1,0:T(8,128)(2,1)}), bf16[1024,2048]{1,0:T(8,128)(2,1)}) %all-gather.11.cloned.1.call-update) | async-done | bytes 4194320 | tf_op jit(solution)/shard_map/all_gather | solution.py:41
  143.8 4.8 %fusion.10 = f32[512,2048]{1,0:T(8,128)S(1)} fusion(bf16[512,1024]{1,0:T(8,128)(2,1)} %all-gather.9.cloned.1.call-done, bf16[1024,2048]{1,0:T(8,128)(2,1)} %all-gather.11.cloned.1.call-done), kind=kOutput, calls=%fused_computation.20 | convolution fusion | flops 2147483648 | bytes 9437184 | tf_op jit(solution)/shard_map/dot_general | solution.py:46
  148.7 5.9 %multiply_convert_fusion = (bf16[512,2048]{1,0:T(8,128)(2,1)}, f32[512,2048]{1,0:T(8,128)}) fusion(f32[512,2048]{1,0:T(8,128)S(1)} %fusion.10, f32[512,128]{1,0:T(8,128)S(1)} %fusion.11, bf16[128,2048]{1,0:T(8,128)(2,1)S(1)} %copy-done), kind=kOutput, calls=%fused_computation.9 | convolution fusion | flops 1622147072 | bytes 11272192 | tf_op jit(solution)/shard_map/dot_general | solution.py:48
  154.6 69.7 %all-gather.7.cloned.1.call-done = bf16[2048,1024]{1,0:T(8,128)(2,1)} async-done(((bf16[2048,256]{1,0:T(8,128)(2,1)}), bf16[2048,1024]{1,0:T(8,128)(2,1)}) %all-gather.7.cloned.1.call-update) | async-done | bytes 4194320 | tf_op jit(solution)/shard_map/all_gather | solution.py:58
  224.3 4.7 %fusion.8 = f32[512,2048]{1,0:T(8,128)S(1)} fusion(bf16[512,1024]{1,0:T(8,128)(2,1)S(1)} %copy-done.3, bf16[2048,1024]{1,0:T(8,128)(2,1)} %all-gather.7.cloned.1.call-done), kind=kOutput, calls=%fused_computation.18 | convolution fusion | flops 2147483648 | bytes 9437184 | tf_op jit(solution)/shard_map/td,fd->tf/dot_general | solution.py:55
  229.1 5.1 %fusion.6 = bf16[512,2048]{1,0:T(8,128)(2,1)S(1)} fusion(f32[512,2048]{1,0:T(8,128)S(1)} %copy-done.8, f32[512,2048]{1,0:T(8,128)S(1)} %fusion.8, f32[512,128]{1,0:T(8,128)S(1)} %fusion.9, bf16[2048,128]{1,0:T(8,128)(2,1)S(1)} %copy-done.7), kind=kOutput, calls=%fused_computation.8 | convolution fusion | flops 1632632832 | bytes 11272192 | tf_op jit(solution)/shard_map/dot_general | solution.py:61
  234.1 0.7 fusion.13
  236.9 1.1 pad_maximum_fusion
  238.1 3.1 convolution_multiply_fusion.1
  241.2 3.3 convolution_multiply_fusion
  244.5 27.9 %reduce-scatter.5.cloned.1.call-done = f32[256,128]{1,0:T(8,128)} async-done(((f32[256,1024]{1,0:T(8,128)}), f32[256,128]{1,0:T(8,128)}) %reduce-scatter.5.cloned.1.call-update) | async-done | bytes 131088 | tf_op jit(solution)/shard_map/reduce_scatter | solution.py:84
  272.4 4.5 %fusion.12 = f32[512,1024]{1,0:T(8,128)S(1)} fusion(bf16[512,2048]{1,0:T(8,128)(2,1)S(1)} %fusion.6, bf16[1024,2048]{1,0:T(8,128)(2,1)} %all-gather.11.cloned.1.call-done), kind=kOutput, calls=%fused_computation.22 | convolution fusion | flops 2147483648 | bytes 8388608 | tf_op jit(solution)/shard_map/tf,df->td/dot_general | solution.py:68
  277.0 2.4 multiply_add_fusion.2
  279.4 86.5 %all-reduce.3.cloned.1.call-done = (f32[256,128]{1,0:T(8,128)}, f32[128,2048]{1,0:T(8,128)}, f32[2048,128]{1,0:T(8,128)}) async-done(((f32[256,128]{1,0:T(8,128)}, f32[128,2048]{1,0:T(8,128)}, f32[2048,128]{1,0:T(8,128)}), (f32[256,128]{1,0:T(8,128)}, f32[128,2048]{1,0:T(8,128)}, f32[2048,128]{1,0:T(8,128)})) %all-reduce.3.cloned.1.call-update) | async-done | bytes 2228240 | tf_op jit(solution)/shard_map/psum | solution.py:86
  365.8 1.5 slice_multiply_fusion
  367.4 0.7 copy.13
  368.1 41.8 %reduce-scatter.3.cloned.1.call-done = f32[512,128]{1,0:T(8,128)} async-done(((f32[512,1024]{1,0:T(8,128)}), f32[512,128]{1,0:T(8,128)}) %reduce-scatter.3.cloned.1.call-update) | async-done | bytes 262160 | tf_op jit(solution)/shard_map/reduce_scatter | solution.py:83
  409.9 2.3 copy.17
  412.2 2.3 copy.18
  (35 shorter events, 5.0 us)
Async XLA Ops:
  7.2 141.5 %copy-start = (bf16[128,2048]{1,0:T(8,128)(2,1)S(1)}, bf16[128,2048]{1,0:T(8,128)(2,1)}, u32[]{:S(2)}) copy-start(bf16[128,2048]{1,0:T(8,128)(2,1)} %param.13) | copy-start | bytes 1572868
  7.2 28.9 %all-gather.5.cloned.1.call-start = ((), (), s32[]{:S(2)}) async-start(), calls=%async_computation.2 | async-start | bytes 1179648 | tf_op jit(solution)/shard_map/all_gather | solution.py:39
  7.9 53.6 %all-gather.9.cloned.1.call-start = ((), (), s32[]{:S(2)}) async-start(), calls=%async_computation.4 | async-start | bytes 1179648 | tf_op jit(solution)/shard_map/all_gather | solution.py:38
  8.7 135.2 %all-gather.11.cloned.1.call-start = ((), (), s32[]{:S(2)}) async-start(), calls=%async_computation.5 | async-start | bytes 5242880 | tf_op jit(solution)/shard_map/all_gather | solution.py:41
  9.4 214.9 %all-gather.7.cloned.1.call-start = ((), (), s32[]{:S(2)}) async-start(), calls=%async_computation.3 | async-start | bytes 5242880 | tf_op jit(solution)/shard_map/all_gather | solution.py:58
  10.0 262.4 %reduce-scatter.5.cloned.1.call-start = ((), (), s32[]{:S(2)}) async-start(), calls=%async_computation.7 | async-start | bytes 1179648 | tf_op jit(solution)/shard_map/reduce_scatter | solution.py:84
  63.1 85.5 %copy-start.6 = (f32[512,128]{1,0:T(8,128)}, f32[512,128]{1,0:T(8,128)S(1)}, u32[]{:S(2)}) copy-start(f32[512,128]{1,0:T(8,128)S(1)} %fusion.11) | copy-start | bytes 786436
  148.7 75.6 %copy-start.3 = (bf16[512,1024]{1,0:T(8,128)(2,1)S(1)}, bf16[512,1024]{1,0:T(8,128)(2,1)}, u32[]{:S(2)}) copy-start(bf16[512,1024]{1,0:T(8,128)(2,1)} %all-gather.5.cloned.1.call-done) | copy-start | bytes 3145732
  224.3 4.7 %copy-start.7 = (bf16[2048,128]{1,0:T(8,128)(2,1)S(1)}, bf16[2048,128]{1,0:T(8,128)(2,1)}, u32[]{:S(2)}) copy-start(bf16[2048,128]{1,0:T(8,128)(2,1)} %param.14) | copy-start | bytes 1572868
  224.3 4.7 %copy-start.8 = (f32[512,2048]{1,0:T(8,128)S(1)}, f32[512,2048]{1,0:T(8,128)}, u32[]{:S(2)}) copy-start(f32[512,2048]{1,0:T(8,128)} %get-tuple-element.16) | copy-start | bytes 12582916
  229.0 5.8 %copy-start.1 = (bf16[512,2048]{1,0:T(8,128)(2,1)S(1)}, bf16[512,2048]{1,0:T(8,128)(2,1)}, u32[]{:S(2)}) copy-start(bf16[512,2048]{1,0:T(8,128)(2,1)} %get-tuple-element.15) | copy-start | bytes 6291460
  234.1 1.5 copy-start.5
  234.1 2.1 copy-start.4
  238.0 127.8 %all-reduce.3.cloned.1.call-start = ((), (), s32[]{:S(2)}) async-start(), calls=%async_computation.8 | async-start | bytes 4456448 | tf_op jit(solution)/shard_map/psum | solution.py:86
  238.1 3.1 copy-start.2
  272.4 137.5 %reduce-scatter.3.cloned.1.call-start = ((), (), s32[]{:S(2)}) async-start(), calls=%async_computation.6 | async-start | bytes 2359296 | tf_op jit(solution)/shard_map/reduce_scatter | solution.py:83
Sparse Core Ops, SparseCore 0:
  9.9 26.1 all-gather.4
  38.0 23.4 all-gather.8
  63.1 80.7 all-gather.10
  145.2 79.0 all-gather.6
  238.1 34.1 reduce-scatter.4
  275.4 90.4 all-reduce.2
  369.7 40.1 reduce-scatter.2
where the time goes:
time: 422 us; the launch traced here: 421 us
  waiting for transfers between devices  348 us (82%)
  matrix products  39.9 us (9%)
  between operations  14.3 us (3%)
  blocking collectives  11 us (3%)
  local copies, waits for them, and re-layouts  5.33 us (1%)
    psum x1, waiting for transfers between devices, local(): lax.psum((grad_out_a, grad_in_b, rank_local), 'tok')  86.5 us
    all_gather x1, waiting for transfers between devices, local(): in_rows = lax.all_gather(frozen_in, 'tok', axis=0, tiled=True)  80.7 us
    all_gather x1, waiting for transfers between devices, local(): lax.all_gather(frozen_out, 'tok', axis=1, tiled=True)  69.7 us
    reduce_scatter x1, waiting for transfers between devices, local(): lax.psum_scatter(dx_term, 'hid', scatter_dimension=1, tiled=True)  41.8 us
    reduce_scatter x1, waiting for transfers between devices, local(): lax.psum_scatter(rank_terms, 'hid', scatter_dimension=1, tiled=True)  27.9 us
    all_gather x1, waiting for transfers between devices, local(): lax.all_gather(tokens, 'hid', axis=1, tiled=True)  23.7 us
    all_gather x1, waiting for transfers between devices, local(): lax.all_gather(cotangent, 'hid', axis=1, tiled=True)  15.1 us
    all_gather x1, blocking collectives, local(): in_a_full = lax.all_gather(input_adapter_first, 'hid', axis=0, tiled=True)  11 us
  transfers between devices with their start and end apart: 7, of which 7 were waited for; matrix products, arithmetic and copies ran while one was open for 7% of the time, Pallas kernels for 0%

commit v1 on v0

--- a/solution.py
+++ b/solution.py
@@ -38,7 +38,13 @@
         lax.all_gather(tokens, "hid", axis=1, tiled=True),
         lax.all_gather(cotangent, "hid", axis=1, tiled=True),
     )
-    in_rows = lax.all_gather(frozen_in, "tok", axis=0, tiled=True)
+    size = lax.axis_size("tok")
+    held, blocks = (frozen_in, [frozen_in])
+    for _ in range(size - 1):
+        held = lax.ppermute(held, "tok", [(i, (i + 1) % size) for i in range(size)])
+        blocks.insert(0, held)
+    merged = jnp.concatenate(blocks, axis=0)
+    in_rows = jnp.roll(merged, (lax.axis_index("tok") + 1) * frozen_in.shape[0], axis=0)
     in_a_full = lax.all_gather(input_adapter_first, "hid", axis=0, tiled=True)
     lowrank_input = jnp.dot(full_tokens, in_a_full, preferred_element_type=jnp.float32)
     second_float = input_adapter_second.astype(jnp.float32)

time: 422 us -> 352 us (0.83)
  waiting for transfers between devices: 348 us -> 273 us
  local copies, waits for them, and re-layouts: 5.33 us -> 9.95 us
    all_gather x1 -> x0, waiting for transfers between devices: 80.7 us -> none  [local(): in_rows = lax.all_gather(frozen_in, 'tok', axis=0, tiled=True)]
    ppermute x0 -> x3, waiting for transfers between devices: none -> 76.4 us  [local(): held = lax.ppermute(held, 'tok', [(i, (i + 1) % size) for i in range(size)])]
    all_gather x1, waiting for transfers between devices: 69.7 us -> 40.1 us  [local(): lax.all_gather(frozen_out, 'tok', axis=1, tiled=True)]
    all_gather x1, waiting for transfers between devices: 23.7 us -> 0.01 us  [local(): lax.all_gather(tokens, 'hid', axis=1, tiled=True)]
    all_gather x1, waiting for transfers between devices: 15.1 us -> 0.02 us  [local(): lax.all_gather(cotangent, 'hid', axis=1, tiled=True)]
    unnamed x21 -> x32, local copies, waits for them, and re-layouts: 5.33 us -> 9.85 us
  transfers between devices with their start and end apart: 7 -> 9, of which waited for: 7 -> 7; matrix products, arithmetic and copies ran while one was open for 7% -> 9% of each run, Pallas kernels for 0% -> 0%
where the time goes in v1:
time: 352 us; the launch traced here: 351 us
  waiting for transfers between devices  273 us (78%)
  matrix products  38.9 us (11%)
  between operations  14.4 us (4%)
  local copies, waits for them, and re-layouts  9.95 us (3%)
  blocking collectives  9.29 us (3%)
    psum x1, waiting for transfers between devices, local(): lax.psum((grad_out_a, grad_in_b, rank_local), 'tok')  86.4 us
    ppermute x3, waiting for transfers between devices, local(): held = lax.ppermute(held, 'tok', [(i, (i + 1) % size) for i in range(size)])  76.4 us
    reduce_scatter x1, waiting for transfers between devices, local(): lax.psum_scatter(dx_term, 'hid', scatter_dimension=1, tiled=True)  41.7 us
    all_gather x1, waiting for transfers between devices, local(): lax.all_gather(frozen_out, 'tok', axis=1, tiled=True)  40.1 us
    reduce_scatter x1, waiting for transfers between devices, local(): lax.psum_scatter(rank_terms, 'hid', scatter_dimension=1, tiled=True)  26.9 us
    unnamed x32, local copies, waits for them, and re-layouts  9.85 us
    all_gather x1, blocking collectives, local(): in_a_full = lax.all_gather(input_adapter_first, 'hid', axis=0, tiled=True)  9.29 us
  transfers between devices with their start and end apart: 9, of which 7 were waited for; matrix products, arithmetic and copies ran while one was open for 9% of the time, Pallas kernels for 0%

profile of v1, /device:TPU:0, one launch (start us, length us, event | category | flops | bytes accessed | tf_op | source)
XLA Modules:
  0.0 351.4 jit_solution(11604966548931054688)
XLA Ops:
  8.7 3.1 collective-permute-start
  11.9 25.3 %collective-permute-done = bf16[256,2048]{1,0:T(8,128)(2,1)S(1)} collective-permute-done((bf16[256,2048]{1,0:T(8,128)(2,1)}, bf16[256,2048]{1,0:T(8,128)(2,1)S(1)}, u32[]{:S(2)}, u32[]{:S(2)}) %collective-permute-start) | collective-permute-done | bytes 1048608 | tf_op jit(solution)/shard_map/ppermute | solution.py:44
  37.2 26.1 %collective-permute-done.1 = bf16[256,2048]{1,0:T(8,128)(2,1)S(1)} collective-permute-done((bf16[256,2048]{1,0:T(8,128)(2,1)S(1)}, bf16[256,2048]{1,0:T(8,128)(2,1)S(1)}, u32[]{:S(2)}, u32[]{:S(2)}) %collective-permute-start.1) | collective-permute-done | bytes 1048608 | tf_op jit(solution)/shard_map/ppermute | solution.py:44
  63.3 9.3 %all_gather.15 = bf16[1024,128]{1,0:T(8,128)(2,1)S(1)} all-gather(bf16[128,128]{1,0:T(8,128)(2,1)} %param.12), channel_id=1, replica_groups=mesh['tok'=4,'hid'=8] {'hid'}, dimensions={0}, use_global_device_ids=true | all-gather | bytes 294912 | tf_op jit(solution)/shard_map/all_gather | solution.py:48
  72.6 1.7 fusion.20
  74.3 1.7 fusion.19
  76.1 2.9 fusion.21
  79.0 25.0 %collective-permute-done.2 = bf16[256,2048]{1,0:T(8,128)(2,1)} collective-permute-done((bf16[256,2048]{1,0:T(8,128)(2,1)S(1)}, bf16[256,2048]{1,0:T(8,128)(2,1)}, u32[]{:S(2)}, u32[]{:S(2)}) %collective-permute-start.2) | collective-permute-done | bytes 1048608 | tf_op jit(solution)/shard_map/ppermute | solution.py:44
  105.7 1.4 constant_dynamic-update-slice_fusion.3
  107.4 5.4 %multiply_convert_fusion = (bf16[512,2048]{1,0:T(8,128)(2,1)S(1)}, f32[512,2048]{1,0:T(8,128)}) fusion(f32[512,2048]{1,0:T(8,128)S(1)} %fusion.21, bf16[512,1024]{1,0:T(8,128)(2,1)S(1)} %copy-done.2, bf16[2048,2048]{1,0:T(8,128)(2,1)S(1)} %constant_dynamic-update-slice_fusion, s32[]{:T(128)S(6)} %select_n.14), kind=kOutput, calls=%fused_computation.10 | convolution fusion | flops 2159017984 | bytes 15728644 | tf_op jit(solution)/shard_map/dot_general | solution.py:52
  112.8 1.3 copy-done.1
  114.9 1.4 fusion.25
  116.3 40.1 %all-gather.6.cloned.1.call-done = bf16[2048,1024]{1,0:T(8,128)(2,1)} async-done(((bf16[2048,256]{1,0:T(8,128)(2,1)}), bf16[2048,1024]{1,0:T(8,128)(2,1)}) %all-gather.6.cloned.1.call-update) | async-done | bytes 4194320 | tf_op jit(solution)/shard_map/all_gather | solution.py:64
  156.4 4.7 %fusion.18 = f32[512,2048]{1,0:T(8,128)S(1)} fusion(bf16[512,1024]{1,0:T(8,128)(2,1)S(1)} %copy-done.4, bf16[2048,1024]{1,0:T(8,128)(2,1)} %all-gather.6.cloned.1.call-done), kind=kOutput, calls=%fused_computation.32 | convolution fusion | flops 2147483648 | bytes 9437184 | tf_op jit(solution)/shard_map/td,fd->tf/dot_general | solution.py:61
  161.1 5.1 %fusion.6 = bf16[512,2048]{1,0:T(8,128)(2,1)S(1)} fusion(f32[512,2048]{1,0:T(8,128)S(1)} %copy-done.10, f32[512,2048]{1,0:T(8,128)S(1)} %fusion.18, f32[512,128]{1,0:T(8,128)S(1)} %fusion.19, bf16[2048,128]{1,0:T(8,128)(2,1)S(1)} %copy-done), kind=kOutput, calls=%fused_computation.8 | convolution fusion | flops 1632632832 | bytes 11272192 | tf_op jit(solution)/shard_map/dot_general | solution.py:67
  168.8 4.9 %convolution_multiply_fusion = f32[2048,128]{1,0:T(8,128)} fusion(bf16[512,2048]{1,0:T(8,128)(2,1)} %copy-done.1, f32[512,128]{1,0:T(8,128)} %copy-done.8), kind=kOutput, calls=%fused_computation.15 | convolution fusion | flops 1610874880 | bytes 3407872 | tf_op jit(solution)/shard_map/dot_general | solution.py:75
  173.7 2.0 convolution_multiply_fusion.1
  175.7 26.9 %reduce-scatter.5.cloned.1.call-done = f32[256,128]{1,0:T(8,128)} async-done(((f32[256,1024]{1,0:T(8,128)}), f32[256,128]{1,0:T(8,128)}) %reduce-scatter.5.cloned.1.call-update) | async-done | bytes 131088 | tf_op jit(solution)/shard_map/reduce_scatter | solution.py:90
  203.7 6.0 %multiply_add_fusion.1 = f32[512,1024]{1,0:T(8,128)} fusion(f32[512,1024]{1,0:T(8,128)S(1)} %fusion.23, bf16[512,2048]{1,0:T(8,128)(2,1)S(1)} %fusion.6, bf16[2048,2048]{1,0:T(8,128)(2,1)} %copy-done.9, s32[]{:T(128)S(6)} %select_n.14), kind=kOutput, calls=%fused_computation.17 | convolution fusion | flops 2148532224 | bytes 10485764 | tf_op jit(solution)/shard_map/tf,df->td/dot_general | solution.py:74
  209.7 86.4 %all-reduce.3.cloned.1.call-done = (f32[256,128]{1,0:T(8,128)}, f32[128,2048]{1,0:T(8,128)}, f32[2048,128]{1,0:T(8,128)}) async-done(((f32[256,128]{1,0:T(8,128)}, f32[128,2048]{1,0:T(8,128)}, f32[2048,128]{1,0:T(8,128)}), (f32[256,128]{1,0:T(8,128)}, f32[128,2048]{1,0:T(8,128)}, f32[2048,128]{1,0:T(8,128)})) %all-reduce.3.cloned.1.call-update) | async-done | bytes 2228240 | tf_op jit(solution)/shard_map/psum | solution.py:92
  296.1 1.5 slice_multiply_fusion
  298.4 41.7 %reduce-scatter.3.cloned.1.call-done = f32[512,128]{1,0:T(8,128)} async-done(((f32[512,1024]{1,0:T(8,128)}), f32[512,128]{1,0:T(8,128)}) %reduce-scatter.3.cloned.1.call-update) | async-done | bytes 262160 | tf_op jit(solution)/shard_map/reduce_scatter | solution.py:89
  340.0 2.3 copy.26
  342.3 2.3 copy.27
  (50 shorter events, 8.5 us)
Async XLA Ops:
  7.2 107.0 %copy-start = (bf16[2048,128]{1,0:T(8,128)(2,1)S(1)}, bf16[2048,128]{1,0:T(8,128)(2,1)}, u32[]{:S(2)}) copy-start(bf16[2048,128]{1,0:T(8,128)(2,1)} %param.14) | copy-start | bytes 1572868
  7.2 65.5 %all-gather.8.cloned.1.call-start = ((), (), s32[]{:S(2)}) async-start(), calls=%async_computation.4 | async-start | bytes 1179648 | tf_op jit(solution)/shard_map/all_gather | solution.py:38
  7.9 66.4 %all-gather.4.cloned.1.call-start = ((), (), s32[]{:S(2)}) async-start(), calls=%async_computation.2 | async-start | bytes 1179648 | tf_op jit(solution)/shard_map/all_gather | solution.py:39
  8.7 147.7 %all-gather.6.cloned.1.call-start = ((), (), s32[]{:S(2)}) async-start(), calls=%async_computation.3 | async-start | bytes 5242880 | tf_op jit(solution)/shard_map/all_gather | solution.py:64
  8.7 28.5 %collective-permute-start = (bf16[256,2048]{1,0:T(8,128)(2,1)}, bf16[256,2048]{1,0:T(8,128)(2,1)S(1)}, u32[]{:S(2)}, u32[]{:S(2)}) collective-permute-start(bf16[256,2048]{1,0:T(8,128)(2,1)} %param.10), channel_id=1, source_target_pairs={{0,8},{8,16},{16,24},{24,0},{1,9},{9,17},{17,25},{25,1},{2,10},{10... | collective-permute-start | bytes 3145736 | tf_op jit(solution)/shard_map/ppermute | solution.py:44
  11.8 190.8 %reduce-scatter.5.cloned.1.call-start = ((), (), s32[]{:S(2)}) async-start(), calls=%async_computation.6 | async-start | bytes 1179648 | tf_op jit(solution)/shard_map/reduce_scatter | solution.py:90
  37.2 26.1 %collective-permute-start.1 = (bf16[256,2048]{1,0:T(8,128)(2,1)S(1)}, bf16[256,2048]{1,0:T(8,128)(2,1)S(1)}, u32[]{:S(2)}, u32[]{:S(2)}) collective-permute-start(bf16[256,2048]{1,0:T(8,128)(2,1)S(1)} %collective-permute-done), channel_id=1, source_target_pairs={{0,8},{8,16},{16,24},{24,0},{1,9},{9,17},{17,25},{25,1},{2,10},{10... | collective-permute-start | bytes 3145736 | tf_op jit(solution)/shard_map/ppermute | solution.py:44
  63.3 40.7 %collective-permute-start.2 = (bf16[256,2048]{1,0:T(8,128)(2,1)S(1)}, bf16[256,2048]{1,0:T(8,128)(2,1)}, u32[]{:S(2)}, u32[]{:S(2)}) collective-permute-start(bf16[256,2048]{1,0:T(8,128)(2,1)S(1)} %collective-permute-done.1), channel_id=1, source_target_pairs={{0,8},{8,16},{16,24},{24,0},{1,9},{9,17},{17,25},{25,1},{2,10},{10... | collective-permute-start | bytes 3145736 | tf_op jit(solution)/shard_map/ppermute | solution.py:44
  76.1 85.0 %copy-start.8 = (f32[512,128]{1,0:T(8,128)}, f32[512,128]{1,0:T(8,128)S(1)}, u32[]{:S(2)}) copy-start(f32[512,128]{1,0:T(8,128)S(1)} %fusion.19) | copy-start | bytes 786436
  79.0 26.5 %copy-start.5 = (bf16[256,2048]{1,0:T(8,128)(2,1)S(1)}, bf16[256,2048]{1,0:T(8,128)(2,1)}, u32[]{:S(2)}) copy-start(bf16[256,2048]{1,0:T(8,128)(2,1)} %param.10) | copy-start | bytes 3145732
  105.7 1.7 copy-start.2
  107.4 5.4 %copy-start.9 = (bf16[2048,2048]{1,0:T(8,128)(2,1)}, bf16[2048,2048]{1,0:T(8,128)(2,1)S(1)}, u32[]{:S(2)}) copy-start(bf16[2048,2048]{1,0:T(8,128)(2,1)S(1)} %constant_dynamic-update-slice_fusion) | copy-start | bytes 25165828
  107.4 7.5 %copy-start.4 = (bf16[512,1024]{1,0:T(8,128)(2,1)S(1)}, bf16[512,1024]{1,0:T(8,128)(2,1)}, u32[]{:S(2)}) copy-start(bf16[512,1024]{1,0:T(8,128)(2,1)} %all-gather.4.cloned.1.call-done) | copy-start | bytes 3145732
  112.8 1.3 copy-start.1
  156.4 4.7 %copy-start.10 = (f32[512,2048]{1,0:T(8,128)S(1)}, f32[512,2048]{1,0:T(8,128)}, u32[]{:S(2)}) copy-start(f32[512,2048]{1,0:T(8,128)} %get-tuple-element.16) | copy-start | bytes 12582916
  161.1 5.1 %copy-start.6 = (bf16[128,2048]{1,0:T(8,128)(2,1)S(1)}, bf16[128,2048]{1,0:T(8,128)(2,1)}, u32[]{:S(2)}) copy-start(bf16[128,2048]{1,0:T(8,128)(2,1)} %param.13) | copy-start | bytes 1572868
  161.1 5.8 %copy-start.3 = (bf16[512,1024]{1,0:T(8,128)(2,1)S(1)}, bf16[512,1024]{1,0:T(8,128)(2,1)}, u32[]{:S(2)}) copy-start(bf16[512,1024]{1,0:T(8,128)(2,1)} %all-gather.8.cloned.1.call-done) | copy-start | bytes 3145732
  166.2 1.4 copy-start.7
  168.7 127.4 %all-reduce.3.cloned.1.call-start = ((), (), s32[]{:S(2)}) async-start(), calls=%async_computation.7 | async-start | bytes 4456448 | tf_op jit(solution)/shard_map/psum | solution.py:92
  202.6 137.4 %reduce-scatter.3.cloned.1.call-start = ((), (), s32[]{:S(2)}) async-start(), calls=%async_computation.5 | async-start | bytes 2359296 | tf_op jit(solution)/shard_map/reduce_scatter | solution.py:89
Sparse Core Ops, SparseCore 0:
  9.9 26.1 all-gather.7
  38.0 23.4 all-gather.3
  63.1 93.2 all-gather.5
  168.8 33.7 reduce-scatter.4
  205.6 90.4 all-reduce.2
  299.8 40.1 reduce-scatter.2
